TPU v7x, 32 devices: a whole 2x2x4 slice. The times are simulated.
32 devices in a mesh: batch: 4 (over x, core), centers: 8 (over z, y).
Axes of the slice: x: 2, y: 2, z: 4, core: 2. Of those that a mesh axis runs over, the one named last changes fastest.
Arguments:
- pool_features: float32 [32768, 128], P(('batch', 'centers')), may hold values from -14 to 14
- pool_targets: float32 [32768, 64], P(('batch', 'centers')), may hold values from -6 to 6
- batch_index: int32 [2048], P(('batch', 'centers')), may hold values from 0 to 1023
- centers: float32 [4096, 128], P('centers'), may hold values from -14 to 14
- weights: float32 [4096, 64], P('centers'), as said below
- eig_vectors: float32 [4096, 1024], P(('batch', 'centers')), may hold values from -0.09375 to 0.09375
- eig_scale: float32 [1024], replicated, may hold values from 0.5 to 4
- nys_owner: int32 [4096, 1], P(('batch', 'centers')), may hold values from 0 to 7; in each aligned block of 128 rows (0 to 127, 128 to 255, ...) at most 32 rows name the same one
- nys_offset: int32 [4096], P(('batch', 'centers')), may hold values from 0 to 511
Outputs:
- residual_out: float32 [2048, 64], P(('batch', 'centers'))
- update: float32 [4096, 64], P('centers')
Inputs may be any that keep to these rules, and one draw needn't show every extreme that they name: `nys_owner`: among the 128 rows of one device no owner is named more than 32 times; on some devices one owner is named exactly 32 times. `weights`: every column sums to zero.
All inputs are finite; a program needn't handle non-finite values.
Results may differ from a plain program's by a relative error of at most 0.0003.
Values sent between devices are 32-bit elements; how exact they have to be, the bound alone decides.
A program may use at most 64 MiB of HBM per device.

v0:
```python
import math

import jax
import jax.numpy as jnp
from jax import lax
from jax.sharding import PartitionSpec as P

DEPTH = 3


epsilon = 1e-06
highest = lax.Precision.HIGHEST


def kernel_rows(row_block, center_block, center_norm):
    inner_prod = (
        lax.dot_general(
            row_block,
            center_block,
            (((1,), (1,)), ((), ())),
            precision=highest,
            preferred_element_type=jnp.float32,
        )
        / row_block.shape[1]
    )
    row_norm = jnp.mean(row_block * row_block, axis=1) + epsilon
    norm_scale = jnp.sqrt(row_norm[:, None] * center_norm[None, :])
    sigma_now = inner_prod
    tangent = inner_prod
    for depth_step in range(DEPTH):
        cosine = sigma_now / norm_scale
        arc_angle = jnp.arccos(cosine)
        remain = (math.pi - arc_angle) / math.pi
        sigma_now = (
            norm_scale
            * (jnp.sqrt(1.0 - cosine * cosine) + (math.pi - arc_angle) * cosine)
            / math.pi
        )
        tangent = sigma_now + tangent * remain
    return tangent


def per_device(
    pool_features,
    pool_targets,
    batch_index,
    centers,
    weights,
    eig_vectors,
    eig_scale,
    nys_owner,
    nys_offset,
):
    local_rows = pool_features[batch_index]
    local_targets = pool_targets[batch_index]
    row_count = local_rows.shape[0]
    group_size = lax.axis_size("centers")
    rows_total = row_count * group_size * lax.axis_size("batch")
    center_count = centers.shape[0]
    outputs = weights.shape[1]
    center_norm = jnp.mean(centers * centers, axis=1) + epsilon
    kernel = kernel_rows(
        lax.all_gather(local_rows, "centers", axis=0, tiled=True), centers, center_norm
    )
    partial_pred = jnp.dot(kernel, weights, precision=highest, preferred_element_type=jnp.float32)
    all_targets = lax.all_gather(local_targets, "centers", axis=0, tiled=True)
    prediction = lax.psum(partial_pred, "centers")
    residual = prediction - all_targets
    own_residual = lax.dynamic_slice_in_dim(
        residual, lax.axis_index("centers") * row_count, row_count, 0
    )
    grads_part = lax.dot_general(
        kernel,
        residual,
        (((0,), (0,)), ((), ())),
        precision=highest,
        preferred_element_type=jnp.float32,
    ) / math.sqrt(rows_total)
    grads = lax.psum(grads_part, "batch")
    owner = nys_owner[:, 0]
    slots = max(2, 2 * owner.shape[0] // group_size)
    owner_hot = (owner[:, None] == jnp.arange(group_size, dtype=jnp.int32)[None, :]).astype(
        jnp.int32
    )
    slot_rank = jnp.sum((jnp.cumsum(owner_hot, axis=0) - owner_hot) * owner_hot, axis=1)
    requests = jnp.zeros((group_size, slots), jnp.int32).at[owner, slot_rank].set(nys_offset)
    received = lax.all_to_all(requests, "centers", split_axis=0, concat_axis=0, tiled=True)
    found = grads[received]
    returned = lax.all_to_all(found, "centers", split_axis=0, concat_axis=0, tiled=True)
    picked_grads = returned[owner, slot_rank]
    coeff_part = lax.dot_general(
        eig_vectors,
        picked_grads,
        (((0,), (0,)), ((), ())),
        precision=highest,
        preferred_element_type=jnp.float32,
    )
    coeff = lax.psum(coeff_part, ("batch", "centers"))
    corr_rows = jnp.dot(
        eig_vectors,
        eig_scale[:, None] * coeff,
        precision=highest,
        preferred_element_type=jnp.float32,
    )
    outgoing = (
        jnp.zeros((group_size, slots, outputs), jnp.float32).at[owner, slot_rank].set(corr_rows)
    )
    incoming = lax.all_to_all(outgoing, "centers", split_axis=0, concat_axis=0, tiled=True)
    corr_part = jnp.zeros((center_count, outputs), jnp.float32).at[received].add(incoming)
    correction = lax.psum(corr_part, "batch")
    return (own_residual, correction - grads)


def solution(mesh):
    placed = (
        P(("batch", "centers"), None),
        P(("batch", "centers"), None),
        P(("batch", "centers")),
        P("centers", None),
        P("centers", None),
        P(("batch", "centers"), None),
        P(),
        P(("batch", "centers"), None),
        P(("batch", "centers")),
    )
    return jax.shard_map(
        per_device,
        mesh=mesh,
        in_specs=placed,
        out_specs=(P(("batch", "centers"), None), P("centers", None)),
        check_vma=False,
    )
```

profile of v0, /device:TPU:0, one launch (start us, length us, event | category | flops | bytes accessed | tf_op | source)
XLA Modules:
  0.0 387.0 jit_solution(5106888059048131326)
XLA Ops:
  7.2 0.0 copy-start
  7.2 0.0 copy-start.6
  7.2 0.7 copy-done.6
  7.9 0.1 fusion.4
  8.0 0.2 reduce_window_sum.11
  8.2 0.2 select_reduce_fusion
  8.3 0.0 copy-start.8
  8.4 0.6 broadcast.104
  9.0 0.1 copy-done.8
  9.0 19.9 %scatter_fusion = s32[8,32]{1,0:T(8,128)} fusion(s32[8,32]{1,0:T(8,128)} %broadcast.104, s32[128]{0:T(128)S(1)} %get-tuple-element.8, s32[128]{0:T(128)S(1)} %copy-done.8), kind=kCustom, calls=%fused_computation.4 | custom fusion | bytes 2560 | tf_op jit(solution)/shard_map/scatter | solution.py:86
  28.9 7.4 %all-to-all-start = ((s32[8,1,32]{2,1,0:T(1,128)}), s32[8,1,32]{2,1,0:T(1,128)S(1)}, u32[]{:S(2)}, u32[]{:S(2)}) async-start(s32[8,1,32]{2,1,0:T(1,128)} %bitcast.4), calls=%async_computation | async-start | bytes 8192 | tf_op jit(solution)/shard_map/all_to_all | solution.py:87
  36.3 0.0 all-reduce.5.cloned.1.call-start
  36.4 0.0 copy-done.9
  36.4 0.0 copy-done.3
  36.4 0.1 multiply_reduce_fusion
  36.6 0.0 copy-done.5
  36.6 0.6 gather_fusion
  37.2 31.2 %all-gather = f32[512,128]{1,0:T(8,128)S(1)} all-gather(f32[64,128]{1,0:T(8,128)S(1)} %gather_fusion), channel_id=2, replica_groups=mesh['batch'=4,'centers'=8] {'centers'}, dimensions={0}, use_global_device_ids=true | all-gather | bytes 294912 | tf_op jit(solution)/shard_map/all_gather | solution.py:63
  68.4 0.1 multiply_reduce_fusion.1
  68.6 0.0 copy-start.4
  68.6 8.9 %multiply_add_fusion = f32[512,512]{1,0:T(8,128)S(1)} fusion(f32[512,128]{1,0:T(8,128)S(1)} %all-gather, f32[512,128]{1,0:T(8,128)S(1)} %copy-done.3, f32[512]{0:T(512)S(1)} %multiply_add_fusion.1, f32[512]{0:T(512)S(1)} %multiply_add_fusion.2), kind=kOutput, calls=%fused_computation.11 | convolution fusion | flops 414187520 | bytes 1576960 | tf_op jit(solution)/shard_map/dot_general | solution.py:17
  77.5 0.0 copy-start.2
  77.5 1.8 fusion.8
  79.3 0.0 all-reduce.5.cloned.1.call-update
  79.4 0.0 all-reduce.7.cloned.1.call-start
  79.4 0.2 copy.23
  79.6 0.6 gather_fusion.1
  80.2 30.8 %all-gather.1 = f32[512,64]{1,0:T(8,128)S(1)} all-gather(f32[64,64]{1,0:T(8,128)S(1)} %gather_fusion.1), channel_id=3, replica_groups=mesh['batch'=4,'centers'=8] {'centers'}, dimensions={0}, use_global_device_ids=true | all-gather | bytes 147456 | tf_op jit(solution)/shard_map/all_gather | solution.py:66
  111.1 0.1 copy.24
  111.2 0.0 all-to-all-done
  111.2 0.1 reshape.100
  111.3 39.5 %all-reduce.5.cloned.1.call-done = f32[512,64]{0,1:T(8,128)} async-done(((f32[512,64]{0,1:T(8,128)}), f32[512,64]{0,1:T(8,128)}) %all-reduce.5.cloned.1.call-update) | async-done | bytes 131088 | tf_op jit(solution)/shard_map/psum | solution.py:67
  150.8 0.9 sub.36
  151.7 1.5 convolution_multiply_fusion.1
  153.2 0.0 all-reduce.7.cloned.1.call-update
  153.2 0.0 all-reduce.9.cloned.1.call-start
  153.3 31.3 %all-reduce.7.cloned.1.call-done = f32[512,64]{0,1:T(8,128)} async-done(((f32[512,64]{0,1:T(8,128)}), f32[512,64]{0,1:T(8,128)}) %all-reduce.7.cloned.1.call-update) | async-done | bytes 131088 | tf_op jit(solution)/shard_map/psum | solution.py:79
  184.6 1.0 copy.26
  185.6 0.7 gather_fusion.2
  186.4 0.1 reshape.114
  186.5 12.2 %all_to_all.22 = f32[8,1,2048]{2,1,0:T(1,128)S(1)} all-to-all(f32[8,1,2048]{2,1,0:T(1,128)S(1)} %reshape.114), channel_id=1, replica_groups=mesh['batch'=4,'centers'=8] {'centers'}, dimensions={0} | all-to-all | bytes 131072 | tf_op jit(solution)/shard_map/all_to_all | solution.py:89
  198.7 0.5 broadcast.212
  199.2 0.8 reduce
  200.0 0.1 reshape.115
  200.1 1.2 gather_fusion.3
  201.3 1.1 convolution_bitcast_fusion
  202.5 0.0 all-reduce.9.cloned.1.call-update
  202.5 123.4 %all-reduce.9.cloned.1.call-done = f32[1024,64]{0,1:T(8,128)} async-done(((f32[1024,64]{0,1:T(8,128)}), f32[1024,64]{0,1:T(8,128)}) %all-reduce.9.cloned.1.call-update) | async-done | bytes 262160 | tf_op jit(solution)/shard_map/psum | solution.py:98
  325.9 1.6 convolution_bitcast_fusion.1
  327.5 0.1 copy.27
  327.6 6.9 %scatter_fusion.1 = f32[8,32,64]{2,1,0:T(8,128)S(1)} fusion(f32[8,32,64]{2,1,0:T(8,128)S(1)} %broadcast_in_dim.8, s32[128]{0:T(128)S(1)} %get-tuple-element.8, f32[128,64]{1,0:T(8,128)S(1)} %copy.27), kind=kCustom, calls=%fused_computation.5 | custom fusion | bytes 99328 | tf_op jit(solution)/shard_map/scatter | solution.py:106
  334.5 0.8 reshape.116
  335.3 4.5 %all-to-all-start.2 = ((f32[8,1,2048]{2,1,0:T(1,128)}), f32[8,1,2048]{2,1,0:T(1,128)S(1)}, u32[]{:S(2)}, u32[]{:S(2)}) async-start(f32[8,1,2048]{2,1,0:T(1,128)} %reshape.116), calls=%async_computation.2 | async-start | bytes 131072 | tf_op jit(solution)/shard_map/all_to_all | solution.py:108
  339.8 0.0 all-reduce.11.cloned.1.call-start
  339.9 6.9 %all-to-all-done.2 = f32[8,1,2048]{2,1,0:T(1,128)S(1)} async-done(((f32[8,1,2048]{2,1,0:T(1,128)}), f32[8,1,2048]{2,1,0:T(1,128)S(1)}, u32[]{:S(2)}, u32[]{:S(2)}) %all-to-all-start.2) | async-done | bytes 65568 | tf_op jit(solution)/shard_map/all_to_all | solution.py:108
  346.8 0.8 reduce.1
  347.6 0.1 reshape.117
  347.6 1.7 scatter_custom_fusion.2
  349.4 0.8 copy.28
  350.2 0.0 all-reduce.11.cloned.1.call-update
  350.2 0.1 constant_dynamic-slice_fusion
  350.3 0.7 copy.29
  351.0 27.9 %all-reduce.11.cloned.1.call-done = f32[512,64]{0,1:T(8,128)} async-done(((f32[512,64]{0,1:T(8,128)}), f32[512,64]{0,1:T(8,128)}) %all-reduce.11.cloned.1.call-update) | async-done | bytes 131088 | tf_op jit(solution)/shard_map/psum | solution.py:110
  378.9 1.6 sub.38
  (18 shorter events, 0.1 us)
Async XLA Ops:
  7.2 194.2 %copy-start = (f32[128,1024]{1,0:T(8,128)S(1)}, f32[128,1024]{1,0:T(8,128)}, u32[]{:S(2)}) copy-start(f32[128,1024]{1,0:T(8,128)} %param.14) | copy-start | bytes 1572868
  7.2 0.7 copy-start.6
  8.3 0.7 copy-start.8
  9.0 27.4 %copy-start.3 = (f32[512,128]{1,0:T(8,128)S(1)}, f32[512,128]{1,0:T(8,128)}, u32[]{:S(2)}) copy-start(f32[512,128]{1,0:T(8,128)} %param.12) | copy-start | bytes 786436
  9.0 27.6 %copy-start.5 = (f32[1024,128]{1,0:T(8,128)S(1)}, f32[1024,128]{1,0:T(8,128)}, u32[]{:S(2)}) copy-start(f32[1024,128]{1,0:T(8,128)} %param.9) | copy-start | bytes 1572868
  28.9 7.5 %copy-start.9 = (s32[64]{0:T(128)S(1)}, s32[64]{0:T(128)}, u32[]{:S(2)}) copy-start(s32[64]{0:T(128)} %param.11) | copy-start | bytes 772
  28.9 82.3 %all-to-all-start = ((s32[8,1,32]{2,1,0:T(1,128)}), s32[8,1,32]{2,1,0:T(1,128)S(1)}, u32[]{:S(2)}, u32[]{:S(2)}) async-start(s32[8,1,32]{2,1,0:T(1,128)} %bitcast.4), calls=%async_computation | async-start | bytes 8192 | tf_op jit(solution)/shard_map/all_to_all | solution.py:87
  36.3 114.5 %all-reduce.5.cloned.1.call-start = ((), (), s32[]{:S(2)}) async-start(), calls=%async_computation.3 | async-start | bytes 262144 | tf_op jit(solution)/shard_map/psum | solution.py:67
  68.6 8.9 %copy-start.4 = (f32[512,64]{0,1:T(8,128)S(1)}, f32[512,64]{0,1:T(8,128)}, u32[]{:S(2)}) copy-start(f32[512,64]{0,1:T(8,128)} %param.13) | copy-start | bytes 393220
  77.5 1.9 copy-start.2
  79.4 105.2 %all-reduce.7.cloned.1.call-start = ((), (), s32[]{:S(2)}) async-start(), calls=%async_computation.4 | async-start | bytes 262144 | tf_op jit(solution)/shard_map/psum | solution.py:79
  153.2 172.7 %all-reduce.9.cloned.1.call-start = ((), (), s32[]{:S(2)}) async-start(), calls=%async_computation.5 | async-start | bytes 524288 | tf_op jit(solution)/shard_map/psum | solution.py:98
  202.5 123.4 %copy-start.7 = (f32[1024]{0:T(1024)S(1)}, f32[1024]{0:T(1024)}, u32[]{:S(2)}) copy-start(f32[1024]{0:T(1024)} %param.15) | copy-start | bytes 12292
  335.3 11.4 %all-to-all-start.2 = ((f32[8,1,2048]{2,1,0:T(1,128)}), f32[8,1,2048]{2,1,0:T(1,128)S(1)}, u32[]{:S(2)}, u32[]{:S(2)}) async-start(f32[8,1,2048]{2,1,0:T(1,128)} %reshape.116), calls=%async_computation.2 | async-start | bytes 131072 | tf_op jit(solution)/shard_map/all_to_all | solution.py:108
  339.8 39.1 %all-reduce.11.cloned.1.call-start = ((), (), s32[]{:S(2)}) async-start(), calls=%async_computation.6 | async-start | bytes 262144 | tf_op jit(solution)/shard_map/psum | solution.py:110
  350.2 28.7 %copy-start.1 = (f32[512,64]{0,1:T(8,128)S(1)}, f32[512,64]{0,1:T(8,128)}, u32[]{:S(2)}) copy-start(f32[512,64]{0,1:T(8,128)} %all-reduce.7.cloned.1.call-done) | copy-start | bytes 393220
Sparse Core Ops, SparseCore 0:
  79.5 71.2 all-reduce.4
  153.7 30.8 all-reduce.6
  202.6 123.2 all-reduce.8
  350.3 28.5 all-reduce.10
where the time goes:
time: 388 us; the launch traced here: 387 us
  waiting for transfers between devices  229 us (59%)
  blocking collectives  74.3 us (19%)
  local copies, waits for them, and re-layouts  36 us (9%)
  matrix products  14.9 us (4%)
  between operations  14 us (4%)
  starting transfers between devices  12.1 us (3%)
  other arithmetic  6.61 us (2%)
    psum x1, waiting for transfers between devices, per_device(): coeff = lax.psum(coeff_part, ('batch', 'centers'))  123 us
    psum x1, waiting for transfers between devices, per_device(): prediction = lax.psum(partial_pred, 'centers')  39.5 us
    psum x1, waiting for transfers between devices, per_device(): grads = lax.psum(grads_part, 'batch')  31.3 us
    all_gather x1, blocking collectives, per_device(): lax.all_gather(local_rows, 'centers', axis=0, tiled=True)  31.2 us
    all_gather x1, blocking collectives, per_device(): all_targets = lax.all_gather(local_targets, 'centers', axis=0, tiled=True)  30.8 us
    psum x1, waiting for transfers between devices, per_device(): correction = lax.psum(corr_part, 'batch')  27.9 us
    scatter x1, local copies, waits for them, and re-layouts, per_device(): jnp.zeros((group_size, slots), jnp.int32).at[owner, slot_rank]  19.9 us
    all_to_all x1, blocking collectives, per_device(): lax.all_to_all(found, 'centers', split_axis=0, concat_axis=0, tiled=True)  12.2 us
  transfers between devices with their start and end apart: 6, of which 5 were waited for; matrix products, arithmetic and copies ran while one was open for 3% of the time, Pallas kernels for 0%

commit v1 on v0

v1 whole, which is shorter than its diff:
```python
import functools
import math

import jax
import jax.numpy as jnp
from jax import lax
from jax.experimental import pallas as pl
from jax.experimental.pallas import tpu as pltpu
from jax.sharding import PartitionSpec as P

DEPTH = 3
EPS = 1e-06
HIGH = lax.Precision.HIGHEST
MESH = pl.DeviceIdType.MESH
ACOS = (
    1.5707963050,
    -0.2145988016,
    0.0889789874,
    -0.0501743046,
    0.0308918810,
    -0.0170881256,
    0.0066700901,
    -0.0012624911,
)


def dot(a, b, ca, cb):
    return lax.dot_general(
        a,
        b,
        (((ca,), (cb,)), ((), ())),
        precision=HIGH,
        preferred_element_type=jnp.float32,
    )


def arc_parts(x):
    u = jnp.maximum(1.0 - x, 1e-30)
    poly = jnp.full_like(x, ACOS[-1] / math.pi)
    for a in ACOS[-2::-1]:
        poly = poly * x + a / math.pi
    v = u * (1.0 + x)
    return u * lax.rsqrt(u) * poly, v * lax.rsqrt(v) * (1.0 / math.pi)


def tangent_kernel(cosine):
    arc, sine = arc_parts(jnp.abs(cosine))
    remain = jnp.where(cosine < 0.0, arc, 1.0 - arc)
    prod = remain * cosine
    sigma = sine + prod
    tangent = sigma + prod
    for _ in range(DEPTH - 1):
        arc, sine = arc_parts(sigma)
        remain = 1.0 - arc
        sigma = sine + remain * sigma
        tangent = sigma + tangent * remain
    return tangent


def body(
    nb,
    nc,
    feat,
    targ,
    cen,
    wts,
    eig,
    scale,
    owner,
    offset,
    res_out,
    upd_out,
    feat_all,
    kbuf,
    ppart,
    prx,
    rsend,
    rrx,
    packed,
    eigrx,
    offsend,
    offrx,
    ebar,
    gsend,
    grx,
    gown,
    gall,
    csend,
    crx,
    cown,
    call,
    usend,
    urx,
    uown,
    uall,
    f_s,
    f_r,
    p_s,
    p_r,
    r_s,
    r_r,
    e_s,
    e_r,
    o_s,
    o_r,
    g_s,
    g_r,
    ga_s,
    ga_r,
    c_s,
    c_r,
    ca_s,
    ca_r,
    u_s,
    u_r,
    ua_s,
    ua_r,
):
    b = lax.axis_index("batch")
    c = lax.axis_index("centers")
    n = nb * nc
    me = b * nc + c
    rows, dim = feat.shape
    cdev = cen.shape[0]
    pts = owner.shape[0]
    slots = packed.shape[1] // nc
    qb = packed.shape[2]
    piece = cdev // nb
    rows_total = rows * n

    def copy(src, dst, ssem, rsem, db, dc):
        return pltpu.make_async_remote_copy(
            src_ref=src,
            dst_ref=dst,
            send_sem=ssem,
            recv_sem=rsem,
            device_id=(db, dc),
            device_id_type=MESH,
        )

    barrier = pltpu.get_barrier_semaphore()

    @pl.loop(1, n)
    def _(k):
        d = lax.rem(me + k, n)
        pl.semaphore_signal(
            barrier, inc=1, device_id=(lax.div(d, nc), lax.rem(d, nc)), device_id_type=MESH
        )

    cval = cen[...]
    csq = cval * cval
    ncol = jnp.mean(csq, axis=1, keepdims=True) + EPS
    sb_col = jnp.sqrt(ncol)
    chat = cval / (sb_col * dim)
    wb = wts[...] * sb_col
    sb_row = jnp.sqrt(dot(jnp.full((8, dim), 1.0 / dim, jnp.float32), csq, 1, 1)[0:1] + EPS)
    a = feat[...]
    sa = jnp.sqrt(jnp.mean(a * a, axis=1, keepdims=True) + EPS)

    pl.semaphore_wait(barrier, n - 1)

    def f_copy(k):
        return copy(feat, feat_all.at[c], f_s.at[k], f_r.at[c], b, lax.rem(c + k, nc))

    @pl.loop(1, nc)
    def _(k):
        f_copy(k).start()

    own = owner[...]
    hot = (own == lax.broadcasted_iota(jnp.int32, (pts, nc), 1)).astype(jnp.float32)
    lower = (
        lax.broadcasted_iota(jnp.int32, (pts, pts), 0)
        > lax.broadcasted_iota(jnp.int32, (pts, pts), 1)
    ).astype(jnp.float32)
    rank = jnp.sum(dot(lower, hot, 1, 0) * hot, axis=1, keepdims=True).astype(jnp.int32)
    lanes = lax.broadcasted_iota(jnp.int32, (pts, nc * slots), 1)
    place = (lanes == own * slots + rank).astype(jnp.float32)
    rowsp = dot(place, eig[...], 0, 0)
    for j in range(nb):
        packed[j] = rowsp[:, j * qb : (j + 1) * qb]
    here = (lanes == c * slots + rank).astype(jnp.float32)
    marks = dot(hot * (offset[...].astype(jnp.float32) + 1.0), here, 0, 0)
    for j in range(nc):
        offsend[j] = marks[j : j + 1]

    def e_copy(k):
        d = lax.rem(me + k, n)
        db, dc = lax.div(d, nc), lax.rem(d, nc)
        return copy(
            packed.at[db, pl.ds(pl.multiple_of(dc * slots, slots), slots)],
            eigrx.at[me],
            e_s.at[k],
            e_r.at[me],
            db,
            dc,
        )

    def o_copy(k):
        d = lax.rem(me + k, n)
        db, dc = lax.div(d, nc), lax.rem(d, nc)
        return copy(offsend.at[dc], offrx.at[me], o_s.at[k], o_r.at[me], db, dc)

    @pl.loop(1, n)
    def _(k):
        o_copy(k).start()
        e_copy(k).start()

    eigrx[me] = packed[b, pl.ds(pl.multiple_of(c * slots, slots), slots)]
    offrx[me] = offsend[c]

    def block(av):
        na = jnp.mean(av * av, axis=1, keepdims=True) + EPS
        k = tangent_kernel(dot(av * lax.rsqrt(na), chat, 1, 1))
        return k, dot(k, wb, 1, 0)

    kown, pown = block(a)
    kbuf[c] = kown
    prx[c] = pown

    def p_copy(k):
        s = lax.rem(c - k + nc, nc)
        return copy(ppart.at[s], prx.at[c], p_s.at[k], p_r.at[c], b, s)

    @pl.loop(1, nc)
    def _(k):
        s = lax.rem(c - k + nc, nc)
        copy(feat, feat_all.at[s], f_s.at[k], f_r.at[s], b, s).wait_recv()
        kv, pv = block(feat_all[s])
        kbuf[s] = kv
        ppart[s] = pv
        p_copy(k).start()

    @pl.loop(1, nc)
    def _(k):
        s = lax.rem(c + k, nc)
        copy(ppart.at[s], prx.at[s], p_s.at[k], p_r.at[s], b, s).wait_recv()

    pred = prx[0]
    for j in range(1, nc):
        pred = pred + prx[j]
    resid = pred * sa - targ[...]
    rs = resid * (sa / math.sqrt(rows_total))
    rsend[...] = rs
    rrx[c] = rs

    def r_copy(k):
        return copy(rsend, rrx.at[c], r_s.at[k], r_r.at[c], b, lax.rem(c + k, nc))

    @pl.loop(1, nc)
    def _(k):
        r_copy(k).start()

    res_out[...] = resid

    @pl.loop(1, nc)
    def _(k):
        s = lax.rem(c - k + nc, nc)
        copy(rsend, rrx.at[s], r_s.at[k], r_r.at[s], b, s).wait_recv()

    outs = rsend.shape[1]
    gt = (
        dot(rrx[...].reshape(nc * rows, outs), kbuf[...].reshape(nc * rows, cdev), 0, 0) * sb_row
    )

    for j in range(nb):
        gsend[j] = gt[:, j * piece : (j + 1) * piece]

    def b_scatter(k, src, dst, ssem, rsem):
        d = lax.rem(b + k, nb)
        return copy(src.at[d], dst.at[b], ssem.at[k], rsem.at[b], d, c)

    def b_gather(k, src, dst, ssem, rsem):
        d = lax.rem(b + k, nb)
        return copy(src, dst.at[b], ssem.at[k], rsem.at[b], d, c)

    def b_wait(k, src, dst, ssem, rsem):
        d = lax.rem(b + k, nb)
        copy(src, dst.at[d], ssem.at[k], rsem.at[d], d, c).wait_recv()

    for k in range(1, nb):
        b_scatter(k, gsend, grx, g_s, g_r).start()
    grx[b] = gsend[b]

    @pl.loop(1, n)
    def _(k):
        s = lax.rem(me - k + n, n)
        copy(offsend.at[0], offrx.at[s], o_s.at[k], o_r.at[s], b, c).wait_recv()
        copy(packed.at[0, pl.ds(0, slots)], eigrx.at[s], e_s.at[k], e_r.at[s], b, c).wait_recv()

    acc = None
    for j in range(nb):
        mark = offrx[j * nc]
        for i in range(1, nc):
            mark = mark + offrx[j * nc + i]
        sel = (
            lax.broadcasted_iota(jnp.int32, (cdev, nc * slots), 0) + 1 == mark.astype(jnp.int32)
        ).astype(jnp.float32)
        part = dot(sel, eigrx[j * nc : (j + 1) * nc].reshape(nc * slots, qb), 1, 0)
        acc = part if acc is None else acc + part
    ebar[...] = acc

    for k in range(1, nb):
        b_wait(k, gown, grx, g_s, g_r)
    gsum = grx[0]
    for j in range(1, nb):
        gsum = gsum + grx[j]
    gown[...] = gsum
    gall[b] = gsum
    for k in range(1, nb):
        b_gather(k, gown, gall, ga_s, ga_r).start()
    for k in range(1, nb):
        b_wait(k, gown, gall, ga_s, ga_r)

    coeff = None
    for j in range(nb):
        part = dot(gall[j], ebar[j * piece : (j + 1) * piece], 1, 0)
        coeff = part if coeff is None else coeff + part
    og = outs // nc
    for j in range(nc):
        csend[j] = coeff[j * og : (j + 1) * og]

    def c_copy(k):
        d = lax.rem(c + k, nc)
        return copy(csend.at[d], crx.at[c], c_s.at[k], c_r.at[c], b, d)

    @pl.loop(1, nc)
    def _(k):
        c_copy(k).start()

    crx[c] = csend[c]

    @pl.loop(1, nc)
    def _(k):
        s = lax.rem(c - k + nc, nc)
        copy(csend.at[0], crx.at[s], c_s.at[k], c_r.at[s], b, s).wait_recv()

    csum = crx[0]
    for j in range(1, nc):
        csum = csum + crx[j]
    csum = csum * scale[b]
    cown[...] = csum
    call[c] = csum

    def ca_copy(k):
        return copy(cown, call.at[c], ca_s.at[k], ca_r.at[c], b, lax.rem(c + k, nc))

    @pl.loop(1, nc)
    def _(k):
        ca_copy(k).start()

    @pl.loop(1, nc)
    def _(k):
        s = lax.rem(c - k + nc, nc)
        copy(cown, call.at[s], ca_s.at[k], ca_r.at[s], b, s).wait_recv()

    scaled = jnp.concatenate([call[j] for j in range(nc)], axis=0)
    for j in range(nb):
        usend[j] = dot(scaled, ebar[j * piece : (j + 1) * piece], 1, 1)
    for k in range(1, nb):
        b_scatter(k, usend, urx, u_s, u_r).start()
    urx[b] = usend[b]
    for k in range(1, nb):
        b_wait(k, uown, urx, u_s, u_r)
    usum = urx[0]
    for j in range(1, nb):
        usum = usum + urx[j]
    usum = usum - gown[...]
    uown[...] = usum
    uall[b] = usum
    for k in range(1, nb):
        b_gather(k, uown, uall, ua_s, ua_r).start()
    for k in range(1, nb):
        b_wait(k, uown, uall, ua_s, ua_r)
    for j in range(nb):
        upd_out[j * piece : (j + 1) * piece] = uall[j].T

    @pl.loop(1, nc)
    def _(k):
        f_copy(k).wait_send()
        p_copy(k).wait_send()
        r_copy(k).wait_send()
        c_copy(k).wait_send()
        ca_copy(k).wait_send()

    @pl.loop(1, n)
    def _(k):
        e_copy(k).wait_send()
        o_copy(k).wait_send()

    for k in range(1, nb):
        b_scatter(k, gsend, grx, g_s, g_r).wait_send()
        b_gather(k, gown, gall, ga_s, ga_r).wait_send()
        b_scatter(k, usend, urx, u_s, u_r).wait_send()
        b_gather(k, uown, uall, ua_s, ua_r).wait_send()


def per_device(
    pool_features,
    pool_targets,
    batch_index,
    centers,
    weights,
    eig_vectors,
    eig_scale,
    nys_owner,
    nys_offset,
):
    nb, nc = lax.axis_size("batch"), lax.axis_size("centers")
    n = nb * nc
    feat = pool_features[batch_index]
    targ = pool_targets[batch_index]
    rows, dim = feat.shape
    outs = targ.shape[1]
    cdev = centers.shape[0]
    pts, q = eig_vectors.shape
    slots = max(2, 2 * pts // nc)
    qb, piece, og = q // nb, cdev // nb, outs // nc
    f32 = jnp.float32
    vm = pltpu.VMEM
    dma = pltpu.SemaphoreType.DMA
    spec = pl.BlockSpec(memory_space=pltpu.VMEM)
    pair = [dma((nc,)), dma((nc,))]
    every = [dma((n,)), dma((n,))]
    quad = [dma((nb,)), dma((nb,))]
    return pl.pallas_call(
        functools.partial(body, nb, nc),
        out_shape=(
            jax.ShapeDtypeStruct((rows, outs), f32),
            jax.ShapeDtypeStruct((cdev, outs), f32),
        ),
        in_specs=[spec] * 8,
        out_specs=(spec, spec),
        scratch_shapes=[
            vm((nc, rows, dim), f32),
            vm((nc, rows, cdev), f32),
            vm((nc, rows, outs), f32),
            vm((nc, rows, outs), f32),
            vm((rows, outs), f32),
            vm((nc, rows, outs), f32),
            vm((nb, nc * slots, qb), f32),
            vm((n, slots, qb), f32),
            vm((nc, 1, nc * slots), f32),
            vm((n, 1, nc * slots), f32),
            vm((cdev, qb), f32),
            vm((nb, outs, piece), f32),
            vm((nb, outs, piece), f32),
            vm((outs, piece), f32),
            vm((nb, outs, piece), f32),
            vm((nc, og, qb), f32),
            vm((nc, og, qb), f32),
            vm((og, qb), f32),
            vm((nc, og, qb), f32),
            vm((nb, outs, piece), f32),
            vm((nb, outs, piece), f32),
            vm((outs, piece), f32),
            vm((nb, outs, piece), f32),
        ]
        + pair * 3
        + every * 2
        + quad * 2
        + pair * 2
        + quad * 2,
        compiler_params=pltpu.CompilerParams(collective_id=0, has_side_effects=True),
    )(
        feat,
        targ,
        centers,
        weights,
        eig_vectors,
        eig_scale.reshape(nb, 1, qb),
        nys_owner,
        nys_offset[:, None],
    )


def solution(mesh):
    placed = (
        P(("batch", "centers"), None),
        P(("batch", "centers"), None),
        P(("batch", "centers")),
        P("centers", None),
        P("centers", None),
        P(("batch", "centers"), None),
        P(),
        P(("batch", "centers"), None),
        P(("batch", "centers")),
    )
    return jax.shard_map(
        per_device,
        mesh=mesh,
        in_specs=placed,
        out_specs=(P(("batch", "centers"), None), P("centers", None)),
        check_vma=False,
    )
```

time: 388 us -> 87 us (0.22)
  waiting for transfers between devices: 229 us -> 0 us
  Pallas kernels: 0 us -> 76.5 us
  blocking collectives: 74.3 us -> 0 us
  local copies, waits for them, and re-layouts: 36 us -> 8.84 us
  matrix products: 14.9 us -> 0 us
  between operations: 14 us -> 0.67 us
  starting transfers between devices: 12.1 us -> 0 us
  other arithmetic: 6.61 us -> 0.72 us
    psum x4 -> x0, waiting for transfers between devices: 222 us -> none  [the longest x1 123 us: per_device(): coeff = lax.psum(coeff_part, ('batch', 'centers'))]
    pallas_call x0 -> x1, Pallas kernels: none -> 76.5 us  [per_device(): pl.pallas_call(functools.partial(body, nb, nc), out_shape=(jax.ShapeDtype...]
    all_gather x2 -> x0, blocking collectives: 62.1 us -> none  [the longest x1 31.2 us: per_device(): lax.all_gather(local_rows, 'centers', axis=0, tiled=True)]
    scatter x2 -> x0, local copies, waits for them, and re-layouts: 26.8 us -> none  [the longest x1 19.9 us: per_device(): jnp.zeros((group_size, slots), jnp.int32).at[owner, slot_rank]]
    dot_general x5 -> x0, matrix products: 14.9 us -> none  [the longest x1 8.91 us: kernel_rows(): lax.dot_general(row_block, center_block, (((1,), (1,)), ((), ())), precis...]
    all_to_all x1 -> x0, blocking collectives: 12.2 us -> none  [per_device(): lax.all_to_all(found, 'centers', split_axis=0, concat_axis=0, tiled=True)]
    all_to_all x2 -> x0, starting transfers between devices: 12 us -> none  [the longest x1 7.44 us: per_device(): lax.all_to_all(requests, 'centers', split_axis=0, concat_axis=0, tiled=True)]
    all_to_all x2 -> x0, waiting for transfers between devices: 6.86 us -> none  [the longest x1 6.86 us: per_device(): lax.all_to_all(outgoing, 'centers', split_axis=0, concat_axis=0, tiled=True)]
  transfers between devices with their start and end apart: 6 -> 0, of which waited for: 5 -> 0; matrix products, arithmetic and copies ran while one was open for 3% -> 0% of each run, Pallas kernels for 0% -> 0%
where the time goes in v1:
time: 87 us; the launch traced here: 86.8 us
  Pallas kernels  76.5 us (88%)
  local copies, waits for them, and re-layouts  8.84 us (10%)
    pallas_call x1, Pallas kernels, per_device(): pl.pallas_call(functools.partial(body, nb, nc), out_shape=(jax.ShapeDtype...  76.5 us
    unnamed x14, local copies, waits for them, and re-layouts  4 us

profile of v1, /device:TPU:0, one launch (start us, length us, event | category | flops | bytes accessed | tf_op | source)
XLA Modules:
  0.0 86.8 jit_solution(652218411899845707)
XLA Ops:
  0.6 0.0 copy-start
  0.6 0.7 compare_select_fusion
  1.4 1.1 %copy.11 = f32[1024,64]{1,0:T(8,128)S(1)} copy(f32[1024,64]{0,1:T(8,128)} %param.10) | data formatting | bytes 524288 | tf_op args[1]
  2.5 1.2 %gather_fusion.1 = f32[64,64]{1,0:T(8,128)} fusion(f32[1024,64]{1,0:T(8,128)S(1)} %copy.11, s32[1024]{0:T(1024)S(1)} %pad_clamp_fusion), kind=kCustom, calls=%fused_computation.1 | custom fusion | bytes 33024 | tf_op jit(solution)/shard_map/gather | solution.py:411
  3.7 0.0 copy-done
  3.7 0.0 copy-start.1
  3.7 1.2 %gather_fusion = f32[64,128]{1,0:T(8,128)} fusion(f32[1024,128]{1,0:T(8,128)S(1)} %copy-done, s32[1024]{0:T(1024)S(1)} %pad_clamp_fusion), kind=kCustom, calls=%fused_computation | custom fusion | bytes 65792 | tf_op jit(solution)/shard_map/gather | solution.py:410
  4.9 0.0 copy-done.1
  4.9 0.0 copy-start.3
  4.9 0.8 copy.12.wts
  5.7 0.0 copy-done.3
  5.7 0.7 copy.13.owner
  6.5 0.0 copy-start.4
  6.5 0.7 copy-done.4
  7.1 0.7 copy.14.offset
  7.9 76.5 %shard_map.104 = (f32[64,64]{1,0:T(8,128)}, f32[512,64]{1,0:T(8,128)}) custom-call(f32[64,128]{1,0:T(8,128)} %gather_fusion, f32[64,64]{1,0:T(8,128)} %gather_fusion.1, f32[512,128]{1,0:T(8,128)} %cen.1, f32[512,64]{1,0:T(8,128)} %copy.12.wts, f32[128,1024]{1,0:T(8,128)} %eig.1, f32[4,1,256]{2,1,0:T(1,128)} %bitcast.2, s32[128,1]{1,0:T(8,128)} %copy.13.owner, ...), custom_call_target="tpu_custom_call" | custom-call | tf_op jit(solution)/shard_map/pallas_call | solution.py:425
  84.4 0.0 copy-start.2
  84.4 1.7 %copy.15 = f32[512,64]{0,1:T(8,128)} copy(f32[512,64]{1,0:T(8,128)} %get-tuple-element.3) | data formatting | bytes 262144 | tf_op jit(solution)/shard_map/pallas_call | solution.py:425
  86.2 0.0 copy-done.2
  86.2 0.6 copy.17
  (1 shorter events, 0.0 us)
Async XLA Ops:
  0.6 3.1 %copy-start = (f32[1024,128]{1,0:T(8,128)S(1)}, f32[1024,128]{1,0:T(8,128)}, u32[]{:S(2)}) copy-start(f32[1024,128]{1,0:T(8,128)} %param.9) | copy-start | bytes 1572868
  3.7 1.2 %copy-start.1 = (f32[512,64]{0,1:T(8,128)S(1)}, f32[512,64]{0,1:T(8,128)}, u32[]{:S(2)}) copy-start(f32[512,64]{0,1:T(8,128)} %param.13) | copy-start | bytes 393220
  4.9 0.8 copy-start.3
  6.5 0.7 copy-start.4
  84.4 1.7 %copy-start.2 = (f32[64,64]{1,0:T(8,128)S(1)}, f32[64,64]{1,0:T(8,128)}, u32[]{:S(2)}) copy-start(f32[64,64]{1,0:T(8,128)} %get-tuple-element.6) | copy-start | bytes 49156

commit v2 on v1

--- a/solution.py
+++ b/solution.py
@@ -60,8 +60,9 @@
 def body(
     nb,
     nc,
-    feat,
-    targ,
+    pool_f,
+    pool_t,
+    index,
     cen,
     wts,
     eig,
@@ -70,6 +71,7 @@
     offset,
     res_out,
     upd_out,
+    feat,
     feat_all,
     kbuf,
     ppart,
@@ -122,7 +124,7 @@
     me = b * nc + c
     rows, dim = feat.shape
     cdev = cen.shape[0]
-    pts = owner.shape[0]
+    pts = owner.shape[1]
     slots = packed.shape[1] // nc
     qb = packed.shape[2]
     piece = cdev // nb
@@ -147,13 +149,17 @@
             barrier, inc=1, device_id=(lax.div(d, nc), lax.rem(d, nc)), device_id_type=MESH
         )
 
+    drawn = (
+        lax.broadcasted_iota(jnp.int32, (pool_f.shape[0], rows), 0) == index[...]
+    ).astype(jnp.float32)
+    feat[...] = dot(drawn, pool_f[...], 0, 0)
     cval = cen[...]
     csq = cval * cval
     ncol = jnp.mean(csq, axis=1, keepdims=True) + EPS
     sb_col = jnp.sqrt(ncol)
     chat = cval / (sb_col * dim)
-    wb = wts[...] * sb_col
     sb_row = jnp.sqrt(dot(jnp.full((8, dim), 1.0 / dim, jnp.float32), csq, 1, 1)[0:1] + EPS)
+    wb = wts[...] * sb_row
     a = feat[...]
     sa = jnp.sqrt(jnp.mean(a * a, axis=1, keepdims=True) + EPS)
 
@@ -167,19 +173,19 @@
         f_copy(k).start()
 
     own = owner[...]
-    hot = (own == lax.broadcasted_iota(jnp.int32, (pts, nc), 1)).astype(jnp.float32)
-    lower = (
+    hot = (own == lax.broadcasted_iota(jnp.int32, (nc, pts), 0)).astype(jnp.float32)
+    upper = (
         lax.broadcasted_iota(jnp.int32, (pts, pts), 0)
-        > lax.broadcasted_iota(jnp.int32, (pts, pts), 1)
+        < lax.broadcasted_iota(jnp.int32, (pts, pts), 1)
     ).astype(jnp.float32)
-    rank = jnp.sum(dot(lower, hot, 1, 0) * hot, axis=1, keepdims=True).astype(jnp.int32)
-    lanes = lax.broadcasted_iota(jnp.int32, (pts, nc * slots), 1)
-    place = (lanes == own * slots + rank).astype(jnp.float32)
-    rowsp = dot(place, eig[...], 0, 0)
+    rank = jnp.sum(dot(hot, upper, 1, 0) * hot, axis=0, keepdims=True).astype(jnp.int32)
+    spots = lax.broadcasted_iota(jnp.int32, (nc * slots, pts), 0)
+    place = (spots == own * slots + rank).astype(jnp.float32)
+    rowsp = dot(place, eig[...], 1, 0)
     for j in range(nb):
         packed[j] = rowsp[:, j * qb : (j + 1) * qb]
-    here = (lanes == c * slots + rank).astype(jnp.float32)
-    marks = dot(hot * (offset[...].astype(jnp.float32) + 1.0), here, 0, 0)
+    here = (spots == c * slots + rank).astype(jnp.float32)
+    marks = dot(hot * (offset[...].astype(jnp.float32) + 1.0), here, 1, 1)
     for j in range(nc):
         offsend[j] = marks[j : j + 1]
 
@@ -208,10 +214,12 @@
     eigrx[me] = packed[b, pl.ds(pl.multiple_of(c * slots, slots), slots)]
     offrx[me] = offsend[c]
 
+    targ = dot(pool_t[...], drawn, 1, 0).T
+
     def block(av):
         na = jnp.mean(av * av, axis=1, keepdims=True) + EPS
         k = tangent_kernel(dot(av * lax.rsqrt(na), chat, 1, 1))
-        return k, dot(k, wb, 1, 0)
+        return k, dot(k, wb, 1, 1)
 
     kown, pown = block(a)
     kbuf[c] = kown
@@ -238,7 +246,7 @@
     pred = prx[0]
     for j in range(1, nc):
         pred = pred + prx[j]
-    resid = pred * sa - targ[...]
+    resid = pred * sa - targ
     rs = resid * (sa / math.sqrt(rows_total))
     rsend[...] = rs
     rrx[c] = rs
@@ -372,7 +380,7 @@
     for k in range(1, nb):
         b_wait(k, uown, uall, ua_s, ua_r)
     for j in range(nb):
-        upd_out[j * piece : (j + 1) * piece] = uall[j].T
+        upd_out[:, j * piece : (j + 1) * piece] = uall[j]
 
     @pl.loop(1, nc)
     def _(k):
@@ -407,10 +415,8 @@
 ):
     nb, nc = lax.axis_size("batch"), lax.axis_size("centers")
     n = nb * nc
-    feat = pool_features[batch_index]
-    targ = pool_targets[batch_index]
-    rows, dim = feat.shape
-    outs = targ.shape[1]
+    rows, dim = batch_index.shape[0], pool_features.shape[1]
+    outs = pool_targets.shape[1]
     cdev = centers.shape[0]
     pts, q = eig_vectors.shape
     slots = max(2, 2 * pts // nc)
@@ -422,15 +428,16 @@
     pair = [dma((nc,)), dma((nc,))]
     every = [dma((n,)), dma((n,))]
     quad = [dma((nb,)), dma((nb,))]
-    return pl.pallas_call(
+    residual, update = pl.pallas_call(
         functools.partial(body, nb, nc),
         out_shape=(
             jax.ShapeDtypeStruct((rows, outs), f32),
-            jax.ShapeDtypeStruct((cdev, outs), f32),
+            jax.ShapeDtypeStruct((outs, cdev), f32),
         ),
-        in_specs=[spec] * 8,
+        in_specs=[spec] * 9,
         out_specs=(spec, spec),
         scratch_shapes=[
+            vm((rows, dim), f32),
             vm((nc, rows, dim), f32),
             vm((nc, rows, cdev), f32),
             vm((nc, rows, outs), f32),
@@ -462,15 +469,17 @@
         + quad * 2,
         compiler_params=pltpu.CompilerParams(collective_id=0, has_side_effects=True),
     )(
-        feat,
-        targ,
+        pool_features,
+        pool_targets.T,
+        batch_index[None, :],
         centers,
-        weights,
+        weights.T,
         eig_vectors,
         eig_scale.reshape(nb, 1, qb),
-        nys_owner,
-        nys_offset[:, None],
+        nys_owner.reshape(1, pts),
+        nys_offset[None, :],
     )
+    return (residual, update.T)
 
 
 def solution(mesh):

time: 87 us -> 80.4 us (0.924)
  local copies, waits for them, and re-layouts: 8.84 us -> 2.94 us
    gather x2 -> x0, local copies, waits for them, and re-layouts: 2.38 us -> none  [the longest x1 1.19 us: per_device(): feat = pool_features[batch_index]]
    pallas_call x1 -> x0, local copies, waits for them, and re-layouts: 1.73 us -> none  [per_device(): pl.pallas_call(functools.partial(body, nb, nc), out_shape=(jax.ShapeDtype...]
    unnamed x14 -> x2, local copies, waits for them, and re-layouts: 4 us -> 2.94 us
where the time goes in v2:
time: 80.4 us; the launch traced here: 80.2 us
  Pallas kernels  76.6 us (95%)
  local copies, waits for them, and re-layouts  2.94 us (4%)
    pallas_call x1, Pallas kernels, per_device(): pl.pallas_call(functools.partial(body, nb, nc), out_shape=(jax.ShapeDtype...  76.6 us
    unnamed x2, local copies, waits for them, and re-layouts  2.94 us

profile of v2, /device:TPU:0, one launch (start us, length us, event | category | flops | bytes accessed | tf_op | source)
XLA Modules:
  0.0 80.2 jit_solution(13940876531983188431)
XLA Ops:
  0.6 76.6 %shard_map.104 = (f32[64,64]{1,0:T(8,128)}, f32[64,512]{1,0:T(8,128)}) custom-call(f32[1024,128]{1,0:T(8,128)} %pool_f.1, f32[64,1024]{1,0:T(8,128)} %bitcast.7, s32[1,64]{1,0:T(1,128)} %bitcast.11, f32[512,128]{1,0:T(8,128)} %cen.1, f32[64,512]{1,0:T(8,128)} %bitcast.9, f32[128,1024]{1,0:T(8,128)} %eig.1, f32[4,1,256]{2,1,0:T(1,128)} %bitcast.10, ...), custom_call_target="tpu_custom_call" | custom-call | tf_op jit(solution)/shard_map/pallas_call | solution.py:431
  77.2 1.4 %copy.13 = f32[64,64]{1,0:T(8,128)} copy(f32[64,64]{1,0:T(8,128)} %get-tuple-element.8) | data formatting | bytes 32768
  78.6 1.6 %copy.14 = f32[512,64]{0,1:T(8,128)} copy(f32[512,64]{0,1:T(8,128)} %bitcast.8) | data formatting | bytes 262144

commit v3 on v2

--- a/solution.py
+++ b/solution.py
@@ -12,6 +12,7 @@
 EPS = 1e-06
 HIGH = lax.Precision.HIGHEST
 MESH = pl.DeviceIdType.MESH
+FIRST, EACH, EARLY = 8, 14, 1
 ACOS = (
     1.5707963050,
     -0.2145988016,
@@ -163,15 +164,6 @@
     a = feat[...]
     sa = jnp.sqrt(jnp.mean(a * a, axis=1, keepdims=True) + EPS)
 
-    pl.semaphore_wait(barrier, n - 1)
-
-    def f_copy(k):
-        return copy(feat, feat_all.at[c], f_s.at[k], f_r.at[c], b, lax.rem(c + k, nc))
-
-    @pl.loop(1, nc)
-    def _(k):
-        f_copy(k).start()
-
     own = owner[...]
     hot = (own == lax.broadcasted_iota(jnp.int32, (nc, pts), 0)).astype(jnp.float32)
     upper = (
@@ -189,41 +181,51 @@
     for j in range(nc):
         offsend[j] = marks[j : j + 1]
 
-    def e_copy(k):
-        d = lax.rem(me + k, n)
-        db, dc = lax.div(d, nc), lax.rem(d, nc)
+    eigrx[me] = packed[b, pl.ds(pl.multiple_of(c * slots, slots), slots)]
+    offrx[me] = offsend[c]
+
+    targ = dot(pool_t[...], drawn, 1, 0).T
+
+    def block(av):
+        na = jnp.mean(av * av, axis=1, keepdims=True) + EPS
+        k = tangent_kernel(dot(av * lax.rsqrt(na), chat, 1, 1))
+        return k, dot(k, wb, 1, 1)
+
+    kown, pown = block(a)
+    kbuf[c] = kown
+    prx[c] = pown
+
+    pl.semaphore_wait(barrier, n - 1)
+
+    def f_copy(k):
+        return copy(feat, feat_all.at[c], f_s.at[k], f_r.at[c], b, lax.rem(c + k, nc))
+
+    @pl.loop(1, nc)
+    def _(k):
+        f_copy(k).start()
+
+    def e_copy(t):
+        db, dc = lax.rem(b + lax.div(t, nc), nb), lax.rem(c + lax.rem(t, nc), nc)
         return copy(
             packed.at[db, pl.ds(pl.multiple_of(dc * slots, slots), slots)],
             eigrx.at[me],
-            e_s.at[k],
+            e_s.at[t],
             e_r.at[me],
             db,
             dc,
         )
 
-    def o_copy(k):
-        d = lax.rem(me + k, n)
-        db, dc = lax.div(d, nc), lax.rem(d, nc)
-        return copy(offsend.at[dc], offrx.at[me], o_s.at[k], o_r.at[me], db, dc)
-
-    @pl.loop(1, n)
-    def _(k):
-        o_copy(k).start()
-        e_copy(k).start()
-
-    eigrx[me] = packed[b, pl.ds(pl.multiple_of(c * slots, slots), slots)]
-    offrx[me] = offsend[c]
-
-    targ = dot(pool_t[...], drawn, 1, 0).T
-
-    def block(av):
-        na = jnp.mean(av * av, axis=1, keepdims=True) + EPS
-        k = tangent_kernel(dot(av * lax.rsqrt(na), chat, 1, 1))
-        return k, dot(k, wb, 1, 1)
-
-    kown, pown = block(a)
-    kbuf[c] = kown
-    prx[c] = pown
+    def o_copy(t):
+        db, dc = lax.rem(b + lax.div(t, nc), nb), lax.rem(c + lax.rem(t, nc), nc)
+        return copy(offsend.at[dc], offrx.at[me], o_s.at[t], o_r.at[me], db, dc)
+
+    first = (n - 1) * FIRST // 32
+    each = (n - 1) * EACH // (32 * (nc - 1))
+    last = first + each * (nc - 1)
+
+    @pl.loop(1, 1 + first)
+    def _(t):
+        e_copy(t).start()
 
     def p_copy(k):
         s = lax.rem(c - k + nc, nc)
@@ -237,6 +239,10 @@
         kbuf[s] = kv
         ppart[s] = pv
         p_copy(k).start()
+
+        @pl.loop(0, each)
+        def _(t):
+            e_copy(1 + first + (k - 1) * each + t).start()
 
     @pl.loop(1, nc)
     def _(k):
@@ -258,6 +264,14 @@
     def _(k):
         r_copy(k).start()
 
+    @pl.loop(1, n)
+    def _(t):
+        o_copy(t).start()
+
+    @pl.loop(1 + last, n)
+    def _(t):
+        e_copy(t).start()
+
     res_out[...] = resid
 
     @pl.loop(1, nc)
@@ -289,23 +303,27 @@
         b_scatter(k, gsend, grx, g_s, g_r).start()
     grx[b] = gsend[b]
 
-    @pl.loop(1, n)
-    def _(k):
-        s = lax.rem(me - k + n, n)
-        copy(offsend.at[0], offrx.at[s], o_s.at[k], o_r.at[s], b, c).wait_recv()
-        copy(packed.at[0, pl.ds(0, slots)], eigrx.at[s], e_s.at[k], e_r.at[s], b, c).wait_recv()
-
-    acc = None
-    for j in range(nb):
-        mark = offrx[j * nc]
+    def add_group(j):
+        g = lax.rem(b - j + nb, nb) * nc
+
+        @pl.loop(1 if j == 0 else 0, nc)
+        def _(i):
+            s = g + lax.rem(c - i + nc, nc)
+            copy(offsend.at[0], offrx.at[s], o_s.at[i], o_r.at[s], b, c).wait_recv()
+            copy(packed.at[0, pl.ds(0, slots)], eigrx.at[s], e_s.at[i], e_r.at[s], b, c).wait_recv()
+
+        mark = offrx[g]
         for i in range(1, nc):
-            mark = mark + offrx[j * nc + i]
+            mark = mark + offrx[g + i]
         sel = (
             lax.broadcasted_iota(jnp.int32, (cdev, nc * slots), 0) + 1 == mark.astype(jnp.int32)
         ).astype(jnp.float32)
-        part = dot(sel, eigrx[j * nc : (j + 1) * nc].reshape(nc * slots, qb), 1, 0)
-        acc = part if acc is None else acc + part
-    ebar[...] = acc
+        part = dot(sel, eigrx[pl.ds(g, nc)].reshape(nc * slots, qb), 1, 0)
+        ebar[...] = part if j == 0 else ebar[...] + part
+
+    early = min(EARLY, nb)
+    for j in range(early):
+        add_group(j)
 
     for k in range(1, nb):
         b_wait(k, gown, grx, g_s, g_r)
@@ -316,6 +334,8 @@
     gall[b] = gsum
     for k in range(1, nb):
         b_gather(k, gown, gall, ga_s, ga_r).start()
+    for j in range(early, nb):
+        add_group(j)
     for k in range(1, nb):
         b_wait(k, gown, gall, ga_s, ga_r)
 

time: 80.4 us -> 74.3 us (0.924)
  Pallas kernels: 76.6 us -> 70.5 us
    pallas_call x1, Pallas kernels: 76.6 us -> 70.5 us  [per_device(): pl.pallas_call(functools.partial(body, nb, nc), out_shape=(jax.ShapeDtype...]
where the time goes in v3:
time: 74.3 us; the launch traced here: 74.1 us
  Pallas kernels  70.5 us (95%)
  local copies, waits for them, and re-layouts  2.94 us (4%)
    pallas_call x1, Pallas kernels, per_device(): pl.pallas_call(functools.partial(body, nb, nc), out_shape=(jax.ShapeDtype...  70.5 us
    unnamed x2, local copies, waits for them, and re-layouts  2.94 us

profile of v3, /device:TPU:0, one launch (start us, length us, event | category | flops | bytes accessed | tf_op | source)
XLA Modules:
  0.0 74.1 jit_solution(6475768701599798200)
XLA Ops:
  0.6 70.5 %shard_map.104 = (f32[64,64]{1,0:T(8,128)}, f32[64,512]{1,0:T(8,128)}) custom-call(f32[1024,128]{1,0:T(8,128)} %pool_f.1, f32[64,1024]{1,0:T(8,128)} %bitcast.7, s32[1,64]{1,0:T(1,128)} %bitcast.11, f32[512,128]{1,0:T(8,128)} %cen.1, f32[64,512]{1,0:T(8,128)} %bitcast.9, f32[128,1024]{1,0:T(8,128)} %eig.1, f32[4,1,256]{2,1,0:T(1,128)} %bitcast.10, ...), custom_call_target="tpu_custom_call" | custom-call | tf_op jit(solution)/shard_map/pallas_call | solution.py:451
  71.2 1.4 %copy.13 = f32[64,64]{1,0:T(8,128)} copy(f32[64,64]{1,0:T(8,128)} %get-tuple-element.8) | data formatting | bytes 32768
  72.5 1.6 %copy.14 = f32[512,64]{0,1:T(8,128)} copy(f32[512,64]{0,1:T(8,128)} %bitcast.8) | data formatting | bytes 262144

commit v4 on v3

--- a/solution.py
+++ b/solution.py
@@ -12,7 +12,7 @@
 EPS = 1e-06
 HIGH = lax.Precision.HIGHEST
 MESH = pl.DeviceIdType.MESH
-FIRST, EACH, EARLY = 8, 14, 1
+FIRST, EACH, EARLY = 16, 0, 1
 ACOS = (
     1.5707963050,
     -0.2145988016,
@@ -33,6 +33,29 @@
         precision=HIGH,
         preferred_element_type=jnp.float32,
     )
+
+
+def pick(onehot, x):
+    low = jnp.bfloat16
+    hi = x.astype(low)
+    rest = x - hi.astype(jnp.float32)
+    mid = rest.astype(low)
+    parts = (rest - mid.astype(jnp.float32)).astype(low), mid, hi
+    total = None
+    for p in parts:
+        part = jnp.dot(onehot, p, preferred_element_type=jnp.float32)
+        total = part if total is None else total + part
+    return total
+
+
+def fold(x):
+    h = x.shape[0] // 2
+    return jnp.concatenate([x[:h], x[h:]], axis=1)
+
+
+def unfold(x):
+    h = x.shape[1] // 2
+    return jnp.concatenate([x[:, :h], x[:, h:]], axis=0)
 
 
 def arc_parts(x):
@@ -189,7 +212,7 @@
     def block(av):
         na = jnp.mean(av * av, axis=1, keepdims=True) + EPS
         k = tangent_kernel(dot(av * lax.rsqrt(na), chat, 1, 1))
-        return k, dot(k, wb, 1, 1)
+        return k, fold(dot(k, wb, 1, 1))
 
     kown, pown = block(a)
     kbuf[c] = kown
@@ -252,10 +275,11 @@
     pred = prx[0]
     for j in range(1, nc):
         pred = pred + prx[j]
-    resid = pred * sa - targ
+    resid = unfold(pred) * sa - targ
     rs = resid * (sa / math.sqrt(rows_total))
-    rsend[...] = rs
-    rrx[c] = rs
+    folded = fold(rs)
+    rsend[...] = folded
+    rrx[c] = folded
 
     def r_copy(k):
         return copy(rsend, rrx.at[c], r_s.at[k], r_r.at[c], b, lax.rem(c + k, nc))
@@ -279,9 +303,10 @@
         s = lax.rem(c - k + nc, nc)
         copy(rsend, rrx.at[s], r_s.at[k], r_r.at[s], b, s).wait_recv()
 
-    outs = rsend.shape[1]
+    outs = res_out.shape[1]
+    every = jnp.concatenate([unfold(rrx[j]) for j in range(nc)], axis=0)
     gt = (
-        dot(rrx[...].reshape(nc * rows, outs), kbuf[...].reshape(nc * rows, cdev), 0, 0) * sb_row
+        dot(every, kbuf[...].reshape(nc * rows, cdev), 0, 0) * sb_row
     )
 
     for j in range(nb):
@@ -317,8 +342,8 @@
             mark = mark + offrx[g + i]
         sel = (
             lax.broadcasted_iota(jnp.int32, (cdev, nc * slots), 0) + 1 == mark.astype(jnp.int32)
-        ).astype(jnp.float32)
-        part = dot(sel, eigrx[pl.ds(g, nc)].reshape(nc * slots, qb), 1, 0)
+        ).astype(jnp.float32).astype(jnp.bfloat16)
+        part = pick(sel, eigrx[pl.ds(g, nc)].reshape(nc * slots, qb))
         ebar[...] = part if j == 0 else ebar[...] + part
 
     early = min(EARLY, nb)
@@ -460,10 +485,10 @@
             vm((rows, dim), f32),
             vm((nc, rows, dim), f32),
             vm((nc, rows, cdev), f32),
-            vm((nc, rows, outs), f32),
-            vm((nc, rows, outs), f32),
-            vm((rows, outs), f32),
-            vm((nc, rows, outs), f32),
+            vm((nc, rows // 2, 2 * outs), f32),
+            vm((nc, rows // 2, 2 * outs), f32),
+            vm((rows // 2, 2 * outs), f32),
+            vm((nc, rows // 2, 2 * outs), f32),
             vm((nb, nc * slots, qb), f32),
             vm((n, slots, qb), f32),
             vm((nc, 1, nc * slots), f32),

time: 74.3 us -> 69.1 us (0.930)
  Pallas kernels: 70.5 us -> 65.3 us
    pallas_call x1, Pallas kernels: 70.5 us -> 65.3 us  [per_device(): pl.pallas_call(functools.partial(body, nb, nc), out_shape=(jax.ShapeDtype...]
where the time goes in v4:
time: 69.1 us; the launch traced here: 68.9 us
  Pallas kernels  65.3 us (95%)
  local copies, waits for them, and re-layouts  2.94 us (4%)
    pallas_call x1, Pallas kernels, per_device(): pl.pallas_call(functools.partial(body, nb, nc), out_shape=(jax.ShapeDtype...  65.3 us
    unnamed x2, local copies, waits for them, and re-layouts  2.94 us

profile of v4, /device:TPU:0, one launch (start us, length us, event | category | flops | bytes accessed | tf_op | source)
XLA Modules:
  0.0 68.9 jit_solution(18193320363769937373)
XLA Ops:
  0.6 65.3 %shard_map.104 = (f32[64,64]{1,0:T(8,128)}, f32[64,512]{1,0:T(8,128)}) custom-call(f32[1024,128]{1,0:T(8,128)} %pool_f.1, f32[64,1024]{1,0:T(8,128)} %bitcast.7, s32[1,64]{1,0:T(1,128)} %bitcast.11, f32[512,128]{1,0:T(8,128)} %cen.1, f32[64,512]{1,0:T(8,128)} %bitcast.9, f32[128,1024]{1,0:T(8,128)} %eig.1, f32[4,1,256]{2,1,0:T(1,128)} %bitcast.10, ...), custom_call_target="tpu_custom_call" | custom-call | tf_op jit(solution)/shard_map/pallas_call | solution.py:476
  65.9 1.4 %copy.13 = f32[64,64]{1,0:T(8,128)} copy(f32[64,64]{1,0:T(8,128)} %get-tuple-element.8) | data formatting | bytes 32768
  67.3 1.6 %copy.14 = f32[512,64]{0,1:T(8,128)} copy(f32[512,64]{0,1:T(8,128)} %bitcast.8) | data formatting | bytes 262144
